TPU v7x, 256 devices: a whole 4x4x8 slice. The times are simulated.
256 devices in a mesh: ep: 64 (over y_lo, z, x), fsdp: 4 (over y_hi, core).
Axes of the slice: x: 4, y: 4 (y_hi: 2, y_lo: 2; y = y_hi * 2 + y_lo), z: 8, core: 2. Of those that a mesh axis runs over, the one named last changes fastest.
Arguments:
- tokens: bfloat16 [12288, 4096], P(('ep', 'fsdp')), may hold values from -6 to 6
- expert_ids: int32 [12288, 8], P(('ep', 'fsdp')), may hold values from 0 to 63, all different within a row; in each aligned block of 48 rows (0 to 47, 48 to 95, ...) at most 9 rows name the same one
- gate_values: float32 [12288, 8], P(('ep', 'fsdp')), may hold values from 0.05 to 1
- gate_weight: bfloat16 [64, 4096, 1024], P('ep', None, 'fsdp'), may hold values from -0.09375 to 0.09375
- up_weight: bfloat16 [64, 4096, 1024], P('ep', None, 'fsdp'), may hold values from -0.09375 to 0.09375
- down_weight: bfloat16 [64, 4096, 1024], P('ep', None, 'fsdp'), may hold values from -0.1875 to 0.1875
Outputs:
- mixed: bfloat16 [12288, 4096], P(('ep', 'fsdp'))
Inputs may be any that keep to these rules, and one draw needn't show every extreme that they name: `expert_ids`: each row names 8 different experts. Among the rows of one device's aligned block of 48 tokens no expert is named more than 9 times, and in some blocks one expert is named exactly 9 times.
All inputs are finite; a program needn't handle non-finite values.
Results may differ from a plain program's by a relative error of at most 0.0057.
Values may be sent and summed in bfloat16 or wider, within the bound.
No kernel may reach another device: no remote copies, remote signals or barrier semaphores. Data moves between devices by JAX's collectives and lax.ppermute only.
A program may use at most 128 MiB of HBM per device.

v0:
```python
import jax
import jax.numpy as jnp
from jax import lax
from jax.sharding import PartitionSpec as P


def local(tokens, expert_ids, gate_values, gate_weight, up_weight, down_weight):
    tok_rows, model_width = tokens.shape
    top_count = expert_ids.shape[1]
    groups = lax.axis_size("ep")
    capacity = max(2, min(tok_rows, 3 * tok_rows * top_count // (2 * groups)))
    pair_count = tok_rows * top_count
    flat_ids = expert_ids.reshape(pair_count)
    onehot = (flat_ids[:, None] == jnp.arange(groups, dtype=jnp.int32)[None, :]).astype(jnp.int32)
    earlier = jnp.cumsum(onehot, axis=0) - onehot
    slot_index = jnp.sum(earlier * onehot, axis=1)
    position = flat_ids * capacity + slot_index
    source = jnp.repeat(tokens, top_count, axis=0)
    outgoing = jnp.zeros((groups * capacity, model_width), jnp.bfloat16).at[position].set(source)
    outgoing = outgoing.reshape(groups, capacity, model_width)
    gate_shard = gate_weight[0]
    up_shard = up_weight[0]
    down_shard = down_weight[0]
    arrived = lax.all_to_all(outgoing, "ep", split_axis=0, concat_axis=0, tiled=True)
    routed = arrived.reshape(-1, model_width)
    gate_piece = lax.all_gather(gate_shard, "fsdp", axis=1, tiled=True)
    up_piece = lax.all_gather(up_shard, "fsdp", axis=1, tiled=True)
    down_piece = lax.all_gather(down_shard, "fsdp", axis=1, tiled=True)
    gate_part = jnp.dot(routed, gate_piece, preferred_element_type=jnp.float32)
    up_part = jnp.dot(routed, up_piece, preferred_element_type=jnp.float32)
    hidden = (jax.nn.silu(gate_part) * up_part).astype(jnp.bfloat16)
    running = lax.dot_general(
        hidden, down_piece, (((1,), (1,)), ((), ())), preferred_element_type=jnp.float32
    )
    returned = lax.all_to_all(
        running.astype(jnp.bfloat16).reshape(arrived.shape),
        "ep",
        split_axis=0,
        concat_axis=0,
        tiled=True,
    )
    picked = returned.reshape(groups * capacity, model_width)[position]
    weighted = gate_values.reshape(pair_count, 1) * picked.astype(jnp.float32)
    return jnp.sum(weighted.reshape(tok_rows, top_count, model_width), axis=1).astype(jnp.bfloat16)


def solution(mesh):
    placed = (
        P(("ep", "fsdp"), None),
        P(("ep", "fsdp"), None),
        P(("ep", "fsdp"), None),
        P("ep", None, "fsdp"),
        P("ep", None, "fsdp"),
        P("ep", None, "fsdp"),
    )
    return jax.shard_map(
        local, mesh=mesh, in_specs=placed, out_specs=P(("ep", "fsdp"), None), check_vma=False
    )
```

profile of v0, /device:TPU:14, one launch (start us, length us, event | category | flops | bytes accessed | tf_op | source)
XLA Modules:
  0.0 547.9 jit_solution(15737267802993377565)
XLA Ops:
  6.5 0.7 all-gather.9.cloned.1.call-update
  7.3 0.7 all-gather.11.cloned.1.call-update
  8.1 0.7 all-gather.7.cloned.1.call-update
  8.8 0.1 eq.29
  8.9 0.1 eq.25
  9.0 0.9 reduce-window.6
  9.9 0.2 slice_reduce_fusion
  10.2 0.1 copy.9
  10.3 0.1 mul.38
  10.4 0.1 fusion.21
  10.5 7.7 %scatter_custom_fusion = bf16[576,4096]{1,0:T(8,128)(2,1)} fusion(s32[384]{0:T(512)S(1)} %fusion.23, bf16[]{:T(256)} %constant.6.clone.1, bf16[48,4096]{1,0:T(8,128)(2,1)S(1)} %copy-done), kind=kCustom, calls=%fused_computation.11 | custom fusion | bytes 5111810 | tf_op jit(solution)/shard_map/scatter | solution.py:19
  18.2 8.4 %reshape.74 = bf16[64,9,4096]{2,1,0:T(8,128)(2,1)} reshape(bf16[576,4096]{1,0:T(8,128)(2,1)} %scatter_custom_fusion) | data formatting | bytes 9437184 | tf_op jit(solution)/shard_map/reshape | solution.py:20
  26.7 196.8 %all_to_all.10 = bf16[64,9,4096]{2,1,0:T(8,128)(2,1)} all-to-all(bf16[64,9,4096]{2,1,0:T(8,128)(2,1)} %reshape.74), channel_id=1, replica_groups=mesh['ep'=64,'fsdp'=4] {'ep'}, dimensions={0} | all-to-all | bytes 9437184 | tf_op jit(solution)/shard_map/all_to_all | solution.py:24
  223.5 8.5 %reshape.75 = bf16[576,4096]{1,0:T(8,128)(2,1)} reshape(bf16[64,9,4096]{2,1,0:T(8,128)(2,1)} %all_to_all.10) | data formatting | bytes 9437184 | tf_op jit(solution)/shard_map/reshape | solution.py:25
  232.0 8.8 %fusion.2 = f32[576,1024]{1,0:T(8,128)S(1)} fusion(bf16[576,4096]{1,0:T(8,128)(2,1)} %reshape.75, bf16[1,4096,1024]{2,1,0:T(8,128)(2,1)} %all-gather.9.cloned.1.call-done), kind=kOutput, calls=%fused_computation.4 | convolution fusion | flops 4831838208 | bytes 15466496 | tf_op jit(solution)/shard_map/dot_general | solution.py:30
  240.8 53.3 %all-gather.7.cloned.1.call-done = bf16[1,4096,1024]{2,1,0:T(8,128)(2,1)} async-done(((bf16[1,4096,256]{2,1,0:T(8,128)(2,1)}), bf16[1,4096,1024]{2,1,0:T(8,128)(2,1)}) %all-gather.7.cloned.1.call-update) | async-done | bytes 8388624 | tf_op jit(solution)/shard_map/all_gather | solution.py:26
  294.2 18.2 %fusion.7 = bf16[576,4096]{1,0:T(8,128)(2,1)} fusion(bf16[1,4096,1024]{2,1,0:T(8,128)(2,1)} %all-gather.11.cloned.1.call-done, f32[576,1024]{1,0:T(8,128)S(1)} %fusion.2, bf16[576,4096]{1,0:T(8,128)(2,1)} %reshape.75, bf16[1,4096,1024]{2,1,0:T(8,128)(2,1)} %all-gather.7.cloned.1.call-done), kind=kOutput, calls=%fused_computation.10 | convolution fusion | flops 9669574656 | bytes 28573696 | tf_op jit(solution)/shard_map/dot_general | solution.py:32
  312.3 8.2 %reshape.76 = bf16[64,9,4096]{2,1,0:T(8,128)(2,1)} reshape(bf16[576,4096]{1,0:T(8,128)(2,1)} %fusion.7) | data formatting | bytes 9437184 | tf_op jit(solution)/shard_map/reshape | solution.py:36
  320.5 11.9 %all-to-all-start.1 = ((bf16[64,9,4096]{2,1,0:T(8,128)(2,1)}), bf16[64,9,4096]{2,1,0:T(8,128)(2,1)}, u32[]{:S(2)}, u32[]{:S(2)}) async-start(bf16[64,9,4096]{2,1,0:T(8,128)(2,1)} %reshape.76), calls=%async_computation.1 | async-start | bytes 16777216 | tf_op jit(solution)/shard_map/all_to_all | solution.py:35
  332.4 0.7 copy.8
  333.1 185.2 %all-to-all-done.1 = bf16[64,9,4096]{2,1,0:T(8,128)(2,1)} async-done(((bf16[64,9,4096]{2,1,0:T(8,128)(2,1)}), bf16[64,9,4096]{2,1,0:T(8,128)(2,1)}, u32[]{:S(2)}, u32[]{:S(2)}) %all-to-all-start.1) | async-done | bytes 4718624 | tf_op jit(solution)/shard_map/all_to_all | solution.py:35
  518.3 8.4 %reshape.77 = bf16[576,4096]{1,0:T(8,128)(2,1)} reshape(bf16[64,9,4096]{2,1,0:T(8,128)(2,1)} %all-to-all-done.1) | data formatting | bytes 9437184 | tf_op jit(solution)/shard_map/reshape | solution.py:42
  526.7 10.5 %gather_fusion = bf16[384,4096]{1,0:T(8,128)(2,1)S(1)} fusion(bf16[576,4096]{1,0:T(8,128)(2,1)} %reshape.77, s32[1024]{0:T(1024)S(1)} %pad_clamp_fusion), kind=kCustom, calls=%fused_computation | custom fusion | bytes 6292992 | tf_op jit(solution)/shard_map/gather | solution.py:42
  537.3 4.1 fusion.6
  (19 shorter events, 0.3 us)
Async XLA Ops:
  6.5 4.0 copy-start
  6.5 2.2 copy-start.2
  6.5 225.4 %all-gather.9.cloned.1.call-start = ((), (), s32[]{:S(2)}) async-start(), calls=%async_computation.3 | async-start | bytes 10485760 | tf_op jit(solution)/shard_map/all_gather | solution.py:27
  7.3 233.6 %all-gather.11.cloned.1.call-start = ((), (), s32[]{:S(2)}) async-start(), calls=%async_computation.4 | async-start | bytes 10485760 | tf_op jit(solution)/shard_map/all_gather | solution.py:28
  8.0 286.2 %all-gather.7.cloned.1.call-start = ((), (), s32[]{:S(2)}) async-start(), calls=%async_computation.2 | async-start | bytes 10485760 | tf_op jit(solution)/shard_map/all_gather | solution.py:26
  320.5 11.9 %copy-start.3 = (f32[48,8]{0,1:T(8,128)S(1)}, f32[48,8]{0,1:T(8,128)}, u32[]{:S(2)}) copy-start(f32[48,8]{0,1:T(8,128)} %param.8) | copy-start | bytes 4612
  320.5 197.8 %all-to-all-start.1 = ((bf16[64,9,4096]{2,1,0:T(8,128)(2,1)}), bf16[64,9,4096]{2,1,0:T(8,128)(2,1)}, u32[]{:S(2)}, u32[]{:S(2)}) async-start(bf16[64,9,4096]{2,1,0:T(8,128)(2,1)} %reshape.76), calls=%async_computation.1 | async-start | bytes 16777216 | tf_op jit(solution)/shard_map/all_to_all | solution.py:35
  526.7 14.6 %copy-start.1 = (bf16[48,4096]{1,0:T(8,128)(2,1)S(1)}, bf16[48,4096]{1,0:T(8,128)(2,1)}, u32[]{:S(2)}) copy-start(bf16[48,4096]{1,0:T(8,128)(2,1)} %param.6) | copy-start | bytes 1179652
Sparse Core Ops, SparseCore 0:
  9.1 108.5 all-gather.8
  119.5 105.1 all-gather.10
  226.6 67.5 all-gather.6
where the time goes:
time: 549 us; the launch traced here: 548 us
  waiting for transfers between devices  241 us (44%)
  blocking collectives  197 us (36%)
  local copies, waits for them, and re-layouts  53.1 us (10%)
  matrix products  27 us (5%)
  between operations  13.2 us (2%)
  starting transfers between devices  12 us (2%)
    all_to_all x1, blocking collectives, local(): lax.all_to_all(outgoing, 'ep', split_axis=0, concat_axis=0, tiled=True)  197 us
    all_to_all x1, waiting for transfers between devices, local(): lax.all_to_all(running.astype(jnp.bfloat16).reshape(arrived.shape), 'ep',...  185 us
    all_gather x1, waiting for transfers between devices, local(): gate_piece = lax.all_gather(gate_shard, 'fsdp', axis=1, tiled=True)  53.3 us
    dot_general x1, matrix products, local(): lax.dot_general(hidden, down_piece, (((1,), (1,)), ((), ())), preferred_e...  18.2 us
    all_to_all x1, starting transfers between devices, local(): lax.all_to_all(running.astype(jnp.bfloat16).reshape(arrived.shape), 'ep',...  11.9 us
  transfers between devices with their start and end apart: 4, of which 2 were waited for; matrix products, arithmetic and copies ran while one was open for 7% of the time, Pallas kernels for 0%

commit v1 on v0

--- a/solution.py
+++ b/solution.py
@@ -23,7 +23,9 @@
     down_shard = down_weight[0]
     arrived = lax.all_to_all(outgoing, "ep", split_axis=0, concat_axis=0, tiled=True)
     routed = arrived.reshape(-1, model_width)
-    gate_piece = lax.all_gather(gate_shard, "fsdp", axis=1, tiled=True)
+    gate_piece = jnp.concatenate(
+        lax.all_to_all(jnp.stack([gate_shard] * lax.axis_size("fsdp")), "fsdp", 0, 0), axis=1
+    )
     up_piece = lax.all_gather(up_shard, "fsdp", axis=1, tiled=True)
     down_piece = lax.all_gather(down_shard, "fsdp", axis=1, tiled=True)
     gate_part = jnp.dot(routed, gate_piece, preferred_element_type=jnp.float32)

time: 549 us -> 594 us (1.082)
  waiting for transfers between devices: 241 us -> 454 us
  blocking collectives: 197 us -> 0 us
  starting transfers between devices: 12 us -> 29.5 us
  local copies, waits for them, and re-layouts: 53.1 us -> 60.7 us
    all_to_all x0 -> x2, waiting for transfers between devices: none -> 268 us  [the longest x1 182 us: local(): lax.all_to_all(outgoing, 'ep', split_axis=0, concat_axis=0, tiled=True)]
    all_to_all x1 -> x0, blocking collectives: 197 us -> none  [local(): lax.all_to_all(outgoing, 'ep', split_axis=0, concat_axis=0, tiled=True)]
    all_gather x1 -> x0, waiting for transfers between devices: 53.3 us -> none  [local(): gate_piece = lax.all_gather(gate_shard, 'fsdp', axis=1, tiled=True)]
    all_to_all x0 -> x2, starting transfers between devices: none -> 19.2 us  [the longest x1 13.3 us: local(): lax.all_to_all(outgoing, 'ep', split_axis=0, concat_axis=0, tiled=True)]
    another operation x0 -> x2, local copies, waits for them, and re-layouts: none -> 7.16 us  [the longest x1 4.24 us: local(): jnp.stack([gate_shard] * lax.axis_size('fsdp'))]
  transfers between devices with their start and end apart: 4 -> 5, of which waited for: 2 -> 3; matrix products, arithmetic and copies ran while one was open for 7% -> 8% of each run, Pallas kernels for 0% -> 0%
where the time goes in v1:
time: 594 us; the launch traced here: 592 us
  waiting for transfers between devices  454 us (76%)
  local copies, waits for them, and re-layouts  60.7 us (10%)
  starting transfers between devices  29.5 us (5%)
  matrix products  28.5 us (5%)
  between operations  13.5 us (2%)
    all_to_all x1, waiting for transfers between devices, local(): lax.all_to_all(running.astype(jnp.bfloat16).reshape(arrived.shape), 'ep',...  185 us
    all_to_all x1, waiting for transfers between devices, local(): lax.all_to_all(outgoing, 'ep', split_axis=0, concat_axis=0, tiled=True)  182 us
    all_to_all x1, waiting for transfers between devices, local(): lax.all_to_all(jnp.stack([gate_shard] * lax.axis_size('fsdp')), 'fsdp', 0...  86 us
    dot_general x1, matrix products, local(): lax.dot_general(hidden, down_piece, (((1,), (1,)), ((), ())), preferred_e...  18.6 us
    all_to_all x1, starting transfers between devices, local(): lax.all_to_all(outgoing, 'ep', split_axis=0, concat_axis=0, tiled=True)  13.3 us
  transfers between devices with their start and end apart: 5, of which 3 were waited for; matrix products, arithmetic and copies ran while one was open for 8% of the time, Pallas kernels for 0%

profile of v1, /device:TPU:14, one launch (start us, length us, event | category | flops | bytes accessed | tf_op | source)
XLA Modules:
  0.0 592.0 jit_solution(9462687966520133685)
XLA Ops:
  6.5 0.7 all-gather.5.cloned.1.call-update
  7.3 0.8 copy.10
  8.2 0.9 reduce-window.6
  9.1 0.2 slice_reduce_fusion
  9.4 0.7 broadcast_multiply_fusion
  10.4 7.6 %scatter_custom_fusion = bf16[576,4096]{1,0:T(8,128)(2,1)} fusion(s32[384]{0:T(512)S(1)} %fusion.21, bf16[]{:T(256)} %constant.6.clone.1, bf16[48,4096]{1,0:T(8,128)(2,1)S(1)} %copy-done), kind=kCustom, calls=%fused_computation.9 | custom fusion | bytes 5111810 | tf_op jit(solution)/shard_map/scatter | solution.py:19
  18.0 8.4 %reshape.81 = bf16[64,9,4096]{2,1,0:T(8,128)(2,1)} reshape(bf16[576,4096]{1,0:T(8,128)(2,1)} %scatter_custom_fusion) | data formatting | bytes 9437184 | tf_op jit(solution)/shard_map/reshape | solution.py:20
  26.4 13.3 %all-to-all-start = ((bf16[64,9,4096]{2,1,0:T(8,128)(2,1)}), bf16[64,9,4096]{2,1,0:T(8,128)(2,1)}, u32[]{:S(2)}, u32[]{:S(2)}) async-start(bf16[64,9,4096]{2,1,0:T(8,128)(2,1)} %reshape.81), calls=%async_computation | async-start | bytes 16777216 | tf_op jit(solution)/shard_map/all_to_all | solution.py:24
  39.8 0.7 all-gather.7.cloned.1.call-update
  40.5 2.9 copy.13
  43.4 181.7 %all-to-all-done = bf16[64,9,4096]{2,1,0:T(8,128)(2,1)} async-done(((bf16[64,9,4096]{2,1,0:T(8,128)(2,1)}), bf16[64,9,4096]{2,1,0:T(8,128)(2,1)}, u32[]{:S(2)}, u32[]{:S(2)}) %all-to-all-start) | async-done | bytes 4718624 | tf_op jit(solution)/shard_map/all_to_all | solution.py:24
  225.0 4.2 stack.3
  229.3 5.9 all-to-all-start.1
  235.2 8.4 %reshape.82 = bf16[576,4096]{1,0:T(8,128)(2,1)} reshape(bf16[64,9,4096]{2,1,0:T(8,128)(2,1)} %all-to-all-done) | data formatting | bytes 9437184 | tf_op jit(solution)/shard_map/reshape | solution.py:25
  243.6 86.0 %all-to-all-done.1 = bf16[4,4096,256]{1,2,0:T(8,128)(2,1)} async-done(((bf16[4,4096,256]{1,2,0:T(8,128)(2,1)}), bf16[4,4096,256]{1,2,0:T(8,128)(2,1)}, u32[]{:S(2)}, u32[]{:S(2)}) %all-to-all-start.1) | async-done | bytes 8388640 | tf_op jit(solution)/shard_map/all_to_all | solution.py:27
  329.6 10.0 %fusion.23 = f32[576,1024]{1,0:T(8,128)} fusion(bf16[576,4096]{1,0:T(8,128)(2,1)} %reshape.82, bf16[4096,1024]{0,1:T(8,128)(2,1)} %bitcast.4), kind=kOutput, calls=%fused_computation.29 | convolution fusion | flops 4831838208 | bytes 15466496 | tf_op jit(solution)/shard_map/dot_general | solution.py:31
  339.6 18.6 %fusion.5 = bf16[576,4096]{1,0:T(8,128)(2,1)} fusion(bf16[1,4096,1024]{2,1,0:T(8,128)(2,1)} %all-gather.7.cloned.1.call-done, f32[576,1024]{1,0:T(8,128)} %fusion.23, bf16[576,4096]{1,0:T(8,128)(2,1)} %reshape.82, bf16[1,4096,1024]{2,1,0:T(8,128)(2,1)} %all-gather.5.cloned.1.call-done), kind=kOutput, calls=%fused_computation.8 | convolution fusion | flops 9669574656 | bytes 28573696 | tf_op jit(solution)/shard_map/dot_general | solution.py:34
  358.2 8.2 %reshape.85 = bf16[64,9,4096]{2,1,0:T(8,128)(2,1)} reshape(bf16[576,4096]{1,0:T(8,128)(2,1)} %fusion.5) | data formatting | bytes 9437184 | tf_op jit(solution)/shard_map/reshape | solution.py:38
  366.4 10.3 %all-to-all-start.2 = ((bf16[64,9,4096]{2,1,0:T(8,128)(2,1)}), bf16[64,9,4096]{2,1,0:T(8,128)(2,1)}, u32[]{:S(2)}, u32[]{:S(2)}) async-start(bf16[64,9,4096]{2,1,0:T(8,128)(2,1)} %reshape.85), calls=%async_computation.2 | async-start | bytes 16777216 | tf_op jit(solution)/shard_map/all_to_all | solution.py:37
  376.7 0.7 copy.8
  377.4 184.7 %all-to-all-done.2 = bf16[64,9,4096]{2,1,0:T(8,128)(2,1)} async-done(((bf16[64,9,4096]{2,1,0:T(8,128)(2,1)}), bf16[64,9,4096]{2,1,0:T(8,128)(2,1)}, u32[]{:S(2)}, u32[]{:S(2)}) %all-to-all-start.2) | async-done | bytes 4718624 | tf_op jit(solution)/shard_map/all_to_all | solution.py:37
  562.1 8.4 %reshape.86 = bf16[576,4096]{1,0:T(8,128)(2,1)} reshape(bf16[64,9,4096]{2,1,0:T(8,128)(2,1)} %all-to-all-done.2) | data formatting | bytes 9437184 | tf_op jit(solution)/shard_map/reshape | solution.py:44
  570.6 10.5 %gather_fusion = bf16[384,4096]{1,0:T(8,128)(2,1)S(1)} fusion(bf16[576,4096]{1,0:T(8,128)(2,1)} %reshape.86, s32[1024]{0:T(1024)S(1)} %pad_clamp_fusion), kind=kCustom, calls=%fused_computation | custom fusion | bytes 6292992 | tf_op jit(solution)/shard_map/gather | solution.py:44
  581.1 4.1 fusion.4
  (19 shorter events, 0.6 us)
Async XLA Ops:
  6.5 3.9 copy-start
  6.5 333.1 %all-gather.5.cloned.1.call-start = ((), (), s32[]{:S(2)}) async-start(), calls=%async_computation.3 | async-start | bytes 10485760 | tf_op jit(solution)/shard_map/all_gather | solution.py:29
  26.4 198.6 %all-to-all-start = ((bf16[64,9,4096]{2,1,0:T(8,128)(2,1)}), bf16[64,9,4096]{2,1,0:T(8,128)(2,1)}, u32[]{:S(2)}, u32[]{:S(2)}) async-start(bf16[64,9,4096]{2,1,0:T(8,128)(2,1)} %reshape.81), calls=%async_computation | async-start | bytes 16777216 | tf_op jit(solution)/shard_map/all_to_all | solution.py:24
  39.7 299.9 %all-gather.7.cloned.1.call-start = ((), (), s32[]{:S(2)}) async-start(), calls=%async_computation.4 | async-start | bytes 10485760 | tf_op jit(solution)/shard_map/all_gather | solution.py:30
  229.3 100.3 %all-to-all-start.1 = ((bf16[4,4096,256]{1,2,0:T(8,128)(2,1)}), bf16[4,4096,256]{1,2,0:T(8,128)(2,1)}, u32[]{:S(2)}, u32[]{:S(2)}) async-start(bf16[4,4096,256]{1,2,0:T(8,128)(2,1)} %stack.3), calls=%async_computation.1 | async-start | bytes 16777216 | tf_op jit(solution)/shard_map/all_to_all | solution.py:27
  366.4 10.3 %copy-start.2 = (f32[48,8]{0,1:T(8,128)S(1)}, f32[48,8]{0,1:T(8,128)}, u32[]{:S(2)}) copy-start(f32[48,8]{0,1:T(8,128)} %param.8) | copy-start | bytes 4612
  366.4 195.8 %all-to-all-start.2 = ((bf16[64,9,4096]{2,1,0:T(8,128)(2,1)}), bf16[64,9,4096]{2,1,0:T(8,128)(2,1)}, u32[]{:S(2)}, u32[]{:S(2)}) async-start(bf16[64,9,4096]{2,1,0:T(8,128)(2,1)} %reshape.85), calls=%async_computation.2 | async-start | bytes 16777216 | tf_op jit(solution)/shard_map/all_to_all | solution.py:37
  570.6 14.6 %copy-start.1 = (bf16[48,4096]{1,0:T(8,128)(2,1)S(1)}, bf16[48,4096]{1,0:T(8,128)(2,1)}, u32[]{:S(2)}) copy-start(bf16[48,4096]{1,0:T(8,128)(2,1)} %param.6) | copy-start | bytes 1179652
Sparse Core Ops, SparseCore 0:
  9.1 104.9 all-gather.4
  115.9 124.9 all-gather.6
